TPU v7x, 32 devices: a whole 2x2x4 slice. The times are simulated.
32 devices in a mesh: section: 4 (over z), row: 2 (over x), col: 4 (over y, core).
Axes of the slice: x: 2, y: 2, z: 4, core: 2. Of those that a mesh axis runs over, the one named last changes fastest.
Arguments:
- input_fwd: bfloat16 [4, 256, 2560], P('section', 'col', 'row'), may hold values from -6 to 6
- input_bwd: bfloat16 [4, 256, 2560], P('section', 'col', 'row'), may hold values from -6 to 6
- cotangent: bfloat16 [4, 256, 2560], P('section', 'col', 'row'), may hold values from -0.375 to 0.375
- shared_up: bfloat16 [2560, 16384], P('row', ('col', 'section')), may hold values from -0.125 to 0.125
- shared_down: bfloat16 [16384, 2560], P(('col', 'section'), 'row'), may hold values from -0.046875 to 0.046875
- up_left: bfloat16 [4, 2560, 256], P('section', 'row'), may hold values from -0.125 to 0.125
- up_right: bfloat16 [4, 256, 16384], P('section', None, 'col'), may hold values from -0.1875 to 0.1875
- down_left: bfloat16 [4, 16384, 256], P('section', 'col'), may hold values from -0.046875 to 0.046875
- down_right: bfloat16 [4, 256, 2560], P('section', None, 'row'), may hold values from -0.1875 to 0.1875
Outputs:
- handoff_fwd: bfloat16 [4, 256, 2560], P('section', 'col', 'row')
- handoff_bwd: bfloat16 [4, 256, 2560], P('section', 'col', 'row')
- grad_shared_up: bfloat16 [2560, 16384], P('row', ('col', 'section'))
- grad_shared_down: bfloat16 [16384, 2560], P(('col', 'section'), 'row')
- grad_up_left: float32 [4, 2560, 256], P('section', 'row')
- grad_up_right: float32 [4, 256, 16384], P('section', None, 'col')
- grad_down_left: float32 [4, 16384, 256], P('section', 'col')
- grad_down_right: float32 [4, 256, 2560], P('section', None, 'row')
All inputs are finite; a program needn't handle non-finite values.
Results may differ from a plain program's by a relative error of at most 0.022.
Values may be sent and summed in bfloat16 or wider, within the bound.
A program may use at most 128 MiB of HBM per device.

v0:
```python
import jax
import jax.numpy as jnp
from jax import lax
from jax.sharding import PartitionSpec as P

F32, BF16 = jnp.float32, jnp.bfloat16


def from_behind(block, axis, distance):
    count = lax.axis_size(axis)
    return lax.ppermute(block, axis, [((i - distance) % count, i) for i in range(count)])


def row_sum(part):
    total = part.astype(F32)
    for step in range(1, lax.axis_size("row")):
        total = total + from_behind(part, "row", step).astype(F32)
    return total


def row_gather(block, axis):
    count, me = lax.axis_size("row"), lax.axis_index("row")
    wide = jnp.zeros(block.shape[:axis] + (count * block.shape[axis],) + block.shape[axis + 1 :], block.dtype)
    for step in range(count):
        piece = block if step == 0 else from_behind(block, "row", step)
        origin = (me - step) % count
        wide = lax.dynamic_update_slice_in_dim(wide, piece, origin * block.shape[axis], axis)
    return wide


def mm(spec, left, right):
    return jnp.einsum(spec, left, right, preferred_element_type=F32)


def silu_slope(preact):
    sigma = jax.nn.sigmoid(preact)
    return sigma * (1.0 + preact * (1.0 - sigma))


def local(
    input_fwd,
    input_bwd,
    cotangent,
    shared_up,
    shared_down,
    up_left,
    up_right,
    down_left,
    down_right,
):
    sections, rows = lax.axis_size("section"), lax.axis_size("row")
    section, row = lax.axis_index("section"), lax.axis_index("row")
    own, width = input_fwd.shape[1], input_fwd.shape[2]
    units = shared_up.shape[1]
    share = up_left.shape[2] // rows
    everyone = ("section", "col")
    micro = own * lax.axis_size("col")

    def own_share(block, axis):
        return lax.dynamic_slice_in_dim(block, row * share, share, axis)

    def own_section(tokens):
        return lax.dynamic_slice_in_dim(tokens, section * micro, micro, 0)

    def per_section(tokens):
        return tokens.reshape(sections, micro, tokens.shape[-1])

    x_fwd, x_bwd, cot = input_fwd[0], input_bwd[0], cotangent[0]
    all_bwd = lax.all_gather(x_bwd, everyone, axis=0, tiled=True)
    all_cot = lax.all_gather(cot, everyone, axis=0, tiled=True)
    all_fwd = lax.all_gather(x_fwd, everyone, axis=0, tiled=True)

    din_part = mm("tmd,dr->tmr", jnp.stack([x_fwd, x_bwd]), up_left[0])
    gdout_part = mm("md,rd->mr", cot, down_right[0])
    low_part = jnp.concatenate([din_part, gdout_part[None]]).astype(BF16)
    low = own_share(row_sum(low_part).astype(BF16), 2)
    low_all = lax.all_gather(low, everyone, axis=1, tiled=True)
    din_fwd, din_bwd, gdout = (per_section(low_all[i]) for i in range(3))

    right = lax.all_to_all(own_share(up_right[0], 0), "section", 1, 0, tiled=True)
    right = right.reshape(sections, share, units)
    left = lax.all_to_all(own_share(down_left[0], 0 + 1), "section", 0, 0, tiled=True)
    left = left.reshape(sections, units, share)

    def preact_of(tokens, din):
        part = mm("smd,df->smf", per_section(tokens), shared_up) + mm("smr,srf->smf", din, right)
        return row_sum(part.astype(BF16))

    pre_bwd = preact_of(all_bwd, din_bwd)
    ghid_part = mm("smd,fd->smf", per_section(all_cot), shared_down) + mm("smr,sfr->smf", gdout, left)
    grad_hidden = row_sum(ghid_part.astype(BF16))
    hid_bwd = jax.nn.silu(pre_bwd).astype(BF16)
    gpre = (grad_hidden * silu_slope(pre_bwd)).astype(BF16)
    flat_gpre = gpre.reshape(sections * micro, units)

    gnorm_part = mm("mf,df->md", flat_gpre, shared_up)
    gdin_part = mm("smf,srf->smr", gpre, right).reshape(sections * micro, share)
    back_part = jnp.concatenate([gnorm_part.astype(BF16), gdin_part.astype(BF16)], axis=1)
    back = lax.psum_scatter(back_part, everyone, scatter_dimension=0, tiled=True)
    gdin_own = row_gather(back[:, width:], 1)

    pre_fwd = preact_of(all_fwd, din_fwd)
    hid_fwd = jax.nn.silu(pre_fwd).astype(BF16)
    out_part = mm("mf,fd->md", hid_fwd.reshape(sections * micro, units), shared_down)
    dout_part = [
        mm("smf,sfr->smr", h, left).reshape(sections * micro, share).astype(BF16) for h in (hid_fwd, hid_bwd)
    ]
    ahead_part = jnp.concatenate([out_part.astype(BF16), *dout_part], axis=1)
    ahead = lax.psum_scatter(ahead_part, everyone, scatter_dimension=0, tiled=True)
    dout_own = row_gather(ahead[:, width:].reshape(own, 2, share), 2)

    grad_up = mm("md,mf->df", all_bwd, flat_gpre).astype(BF16)
    grad_down = mm("mf,md->fd", hid_bwd.reshape(sections * micro, units), all_cot).astype(BF16)

    grad_left = mm("smf,smr->sfr", hid_bwd, gdout).astype(BF16).reshape(sections * units, share)
    grad_left = lax.all_to_all(grad_left, "section", 0, 0, tiled=True)
    grad_down_left = row_gather(grad_left, 1).astype(F32)
    grad_right = mm("smr,smf->srf", din_bwd, gpre).astype(BF16).reshape(sections * share, units)
    grad_right = lax.all_to_all(grad_right, "section", 0, 1, tiled=True)
    grad_up_right = row_gather(grad_right, 0).astype(F32)

    grad_input = (
        cot.astype(F32) + back[:, :width].astype(F32) + mm("mr,dr->md", gdin_own, up_left[0])
    )
    handoff_bwd = from_behind(grad_input.astype(BF16)[None], "section", -1)
    gdin_all = lax.all_gather(gdin_own, "col", axis=0, tiled=True)
    grad_up_left = mm("md,mr->dr", own_section(all_bwd), gdin_all)

    out_fwd = (
        x_fwd.astype(F32) + ahead[:, :width].astype(F32) + mm("mr,rd->md", dout_own[:, 0], down_right[0])
    )
    handoff_fwd = from_behind(out_fwd.astype(BF16)[None], "section", 1)
    dout_all = lax.all_gather(dout_own[:, 1], "col", axis=0, tiled=True)
    grad_down_right = mm("mr,md->rd", dout_all, own_section(all_cot))
    return (
        handoff_fwd,
        handoff_bwd,
        grad_up,
        grad_down,
        grad_up_left[None],
        grad_up_right[None],
        grad_down_left[None],
        grad_down_right[None],
    )


def solution(mesh):
    in_specs = (
        P("section", "col", "row"),
        P("section", "col", "row"),
        P("section", "col", "row"),
        P("row", ("col", "section")),
        P(("col", "section"), "row"),
        P("section", "row", None),
        P("section", None, "col"),
        P("section", "col", None),
        P("section", None, "row"),
    )
    out_specs = (
        P("section", "col", "row"),
        P("section", "col", "row"),
        P("row", ("col", "section")),
        P(("col", "section"), "row"),
        P("section", "row", None),
        P("section", None, "col"),
        P("section", "col", None),
        P("section", None, "row"),
    )
    return jax.shard_map(local, mesh=mesh, in_specs=in_specs, out_specs=out_specs, check_vma=False)
```

profile of v0, /device:TPU:0, one launch (start us, length us, event | category | flops | bytes accessed | tf_op | source)
XLA Modules:
  0.0 362.8 jit_solution(5523919161392895789)
XLA Ops:
  11.0 6.3 %all-to-all-start.1 = ((bf16[4,1024,128]{2,1,0:T(8,128)(2,1)}), bf16[4,1024,128]{2,1,0:T(8,128)(2,1)}, u32[]{:S(2)}, u32[]{:S(2)}) async-start(bf16[4,1024,128]{2,1,0:T(8,128)(2,1)} %bitcast.122), calls=%async_computation.1 | async-start | bytes 2097152 | tf_op jit(solution)/shard_map/all_to_all | solution.py:82
  28.0 32.3 %all_gather.19 = bf16[3,1024,128]{2,1,0:T(8,128)(2,1)S(1)} all-gather(bf16[3,64,128]{2,1,0:T(8,128)(2,1)S(1)} %add_convert_fusion.3), channel_id=1, replica_groups=mesh['section'=4,'row'=2,'col'=4] {'section','col'}, dimensions={1}, use_global_device_ids=true | all-gather | bytes 835584 | tf_op jit(solution)/shard_map/all_gather | solution.py:77
  61.2 6.1 %all-to-all-start = ((bf16[128,4,1024]{2,0,1:T(8,128)(2,1)}), bf16[128,4,1024]{2,0,1:T(8,128)(2,1)}, u32[]{:S(2)}, u32[]{:S(2)}) async-start(bf16[128,4,1024]{2,0,1:T(8,128)(2,1)} %copy.21), calls=%async_computation | async-start | bytes 2097152 | tf_op jit(solution)/shard_map/all_to_all | solution.py:80
  70.3 5.4 %fusion.3 = f32[4,256,1024]{2,1,0:T(8,128)S(1)} fusion(bf16[4,256,1280]{2,1,0:T(8,128)(2,1)} %bitcast.135, bf16[1024,1280]{1,0:T(8,128)(2,1)} %param.13), kind=kOutput, calls=%fused_computation.19 | convolution fusion | flops 2684354560 | bytes 9437184 | tf_op jit(solution)/shard_map/smd,fd->smf/dot_general | solution.py:32
  80.5 40.5 %all-gather.10.cloned.1.call-done = bf16[1,1024,1280]{2,1,0:T(8,128)(2,1)} async-done(((bf16[1,64,1280]{2,1,0:T(8,128)(2,1)}), bf16[1,1024,1280]{2,1,0:T(8,128)(2,1)}) %all-gather.10.cloned.1.call-update) | async-done | bytes 2621456 | tf_op jit(solution)/shard_map/all_gather | solution.py:69
  121.0 6.1 %fusion.5 = f32[4,256,1024]{2,1,0:T(8,128)} fusion(bf16[4,256,1280]{2,1,0:T(8,128)(2,1)} %bitcast.136, bf16[1280,1024]{1,0:T(8,128)(2,1)S(1)} %copy-done), kind=kOutput, calls=%fused_computation.21 | convolution fusion | flops 2684354560 | bytes 9437184 | tf_op jit(solution)/shard_map/smd,df->smf/dot_general | solution.py:32
  127.1 4.7 %add_convert_fusion.1 = bf16[4,256,1024]{2,1,0:T(8,128)(2,1)} fusion(f32[4,256,1024]{2,1,0:T(8,128)} %fusion.5, bf16[4,256,128]{2,1,0:T(8,128)(2,1)} %bitcast.128, bf16[128,4,1024]{2,0,1:T(8,128)(2,1)} %all-to-all-done), kind=kOutput, calls=%fused_computation.5 | convolution fusion | flops 270532608 | bytes 7602176 | tf_op jit(solution)/shard_map/smr,srf->smf/dot_general | solution.py:32
  133.2 32.0 %all-gather.8.cloned.1.call-done = bf16[1,1024,1280]{2,1,0:T(8,128)(2,1)} async-done(((bf16[1,64,1280]{2,1,0:T(8,128)(2,1)}), bf16[1,1024,1280]{2,1,0:T(8,128)(2,1)}) %all-gather.8.cloned.1.call-update) | async-done | bytes 2621456 | tf_op jit(solution)/shard_map/all_gather | solution.py:71
  165.3 6.1 %fusion.7 = f32[4,256,1024]{2,1,0:T(8,128)} fusion(bf16[4,256,1280]{2,1,0:T(8,128)(2,1)} %bitcast.137, bf16[1280,1024]{1,0:T(8,128)(2,1)S(1)} %copy-done), kind=kOutput, calls=%fused_computation.23 | convolution fusion | flops 2684354560 | bytes 9437184 | tf_op jit(solution)/shard_map/smd,df->smf/dot_general | solution.py:32
  171.4 8.5 %collective-permute-done.2 = bf16[4,256,1024]{2,1,0:T(8,128)(2,1)} collective-permute-done((bf16[4,256,1024]{2,1,0:T(8,128)(2,1)}, bf16[4,256,1024]{2,1,0:T(8,128)(2,1)}, u32[]{:S(2)}, u32[]{:S(2)}) %collective-permute-start.2) | collective-permute-done | bytes 2097184 | tf_op jit(solution)/shard_map/ppermute | solution.py:11
  179.9 5.7 %multiply_convert_fusion = (bf16[4,256,1024]{2,1,0:T(8,128)(2,1)S(1)}, bf16[4,256,1024]{2,1,0:T(8,128)(2,1)}) fusion(bf16[4,256,1024]{2,1,0:T(8,128)(2,1)} %collective-permute-done.5, bf16[4,256,1024]{2,1,0:T(8,128)(2,1)} %add_convert_fusion, bf16[4,256,1024]{2,1,0:T(8,128)(2,1)} %collective-permute-done.2, bf16[4,256,1024]{2,1,0:T(8,128)(2,1)} %add_convert_fusion.1), kind=kLoop, calls=%fused_computation | loop fusion | flops 17825792 | bytes 12582912 | tf_op jit(solution)/shard_map/convert_element_type | solution.py:93
  199.7 4.4 %all-to-all-start.2 = ((bf16[4,128,1024]{2,1,0:T(8,128)(2,1)}), bf16[4,128,1024]{2,1,0:T(8,128)(2,1)}, u32[]{:S(2)}, u32[]{:S(2)}) async-start(bf16[4,128,1024]{2,1,0:T(8,128)(2,1)} %convolution_convert_fusion.5), calls=%async_computation.4 | async-start | bytes 2097152 | tf_op jit(solution)/shard_map/all_to_all | solution.py:119
  204.2 3.7 %convolution_convert_fusion.4 = bf16[4,1024,128]{2,1,0:T(8,128)(2,1)} fusion(bf16[4,256,1024]{2,1,0:T(8,128)(2,1)} %get-tuple-element.25, bf16[4,256,128]{2,1,0:T(8,128)(2,1)S(1)} %bitcast.127), kind=kOutput, calls=%fused_computation.31 | convolution fusion | flops 268959744 | bytes 3407872 | tf_op jit(solution)/shard_map/smf,smr->sfr/dot_general | solution.py:32
  209.9 34.0 %collective-permute-done.1 = bf16[4,256,1024]{2,1,0:T(8,128)(2,1)} collective-permute-done((bf16[4,256,1024]{2,1,0:T(8,128)(2,1)S(1)}, bf16[4,256,1024]{2,1,0:T(8,128)(2,1)}, u32[]{:S(2)}, u32[]{:S(2)}) %collective-permute-start.1) | collective-permute-done | bytes 2097184 | tf_op jit(solution)/shard_map/ppermute | solution.py:11
  251.2 4.2 %all-to-all-start.3 = ((bf16[4,1024,128]{2,1,0:T(8,128)(2,1)}), bf16[4,1024,128]{2,1,0:T(8,128)(2,1)}, u32[]{:S(2)}, u32[]{:S(2)}) async-start(bf16[4,1024,128]{2,1,0:T(8,128)(2,1)} %convolution_convert_fusion.4), calls=%async_computation.5 | async-start | bytes 2097152 | tf_op jit(solution)/shard_map/all_to_all | solution.py:116
  260.0 7.0 %fusion = bf16[1280,1024]{0,1:T(8,128)(2,1)} fusion(bf16[1024,1024]{1,0:T(8,128)(2,1)} %bitcast.121, bf16[1,1024,1280]{2,1,0:T(8,128)(2,1)} %all-gather.10.cloned.1.call-done), kind=kOutput, calls=%fused_computation.12 | convolution fusion | flops 2685665280 | bytes 7340032 | tf_op jit(solution)/shard_map/md,mf->df/dot_general | solution.py:32
  270.6 9.5 %all-to-all-done.3 = bf16[4,1024,128]{2,1,0:T(8,128)(2,1)} async-done(((bf16[4,1024,128]{2,1,0:T(8,128)(2,1)}), bf16[4,1024,128]{2,1,0:T(8,128)(2,1)}, u32[]{:S(2)}, u32[]{:S(2)}) %all-to-all-start.3) | async-done | bytes 1048608 | tf_op jit(solution)/shard_map/all_to_all | solution.py:116
  281.7 6.0 %convolution_convert_fusion = bf16[1024,1280]{1,0:T(8,128)(2,1)} fusion(bf16[1024,1024]{1,0:T(8,128)(2,1)S(1)} %bitcast.119, bf16[1,1024,1280]{2,1,0:T(8,128)(2,1)} %all-gather.12.cloned.1.call-done), kind=kOutput, calls=%fused_computation.8 | convolution fusion | flops 2685665280 | bytes 7340032 | tf_op jit(solution)/shard_map/mf,md->fd/dot_general | solution.py:32
  287.7 4.5 %copy.30 = bf16[1280,1024]{1,0:T(8,128)(2,1)} copy(bf16[1280,1024]{0,1:T(8,128)(2,1)} %fusion) | data formatting | bytes 5242880
  300.9 14.5 %collective-permute-done.9 = bf16[4096,128]{1,0:T(8,128)(2,1)} collective-permute-done((bf16[4096,128]{1,0:T(8,128)(2,1)}, bf16[4096,128]{1,0:T(8,128)(2,1)}, u32[]{:S(2)}, u32[]{:S(2)}) %collective-permute-start.9) | collective-permute-done | bytes 1048608 | tf_op jit(solution)/shard_map/ppermute | solution.py:11
  324.1 4.0 %broadcast_in_dim.57 = f32[1,4096,256]{2,1,0:T(8,128)} convert(bf16[1,4096,256]{2,1,0:T(8,128)(2,1)} %bitcast_dynamic-update-slice_fusion) | non-fusion elementwise | flops 1048576 | bytes 6291456 | tf_op jit(solution)/shard_map/broadcast_in_dim | solution.py:142
  328.5 3.5 collective-permute-start.7
  332.0 5.4 %all_gather.22 = bf16[256,256]{1,0:T(8,128)(2,1)S(1)} all-gather(bf16[64,256]{1,0:T(8,128)(2,1)S(1)} %constant_dynamic-update-slice_fusion.2), channel_id=1, replica_groups=mesh['section'=4,'row'=2,'col'=4] {'col'}, dimensions={0}, use_global_device_ids=true | all-gather | bytes 163840 | tf_op jit(solution)/shard_map/all_gather | solution.py:126
  346.0 5.4 %all-gather.3 = bf16[256,1,256]{2,0,1:T(8,128)(2,1)S(1)} all-gather(bf16[64,1,256]{2,0,1:T(8,128)(2,1)S(1)} %slice.44), channel_id=5, replica_groups=mesh['section'=4,'row'=2,'col'=4] {'col'}, dimensions={0}, use_global_device_ids=true | all-gather | bytes 163840 | tf_op jit(solution)/shard_map/all_gather | solution.py:133
  (114 shorter events, 88.6 us)
Async XLA Ops:
  7.2 113.8 %copy-start = (bf16[1280,1024]{1,0:T(8,128)(2,1)S(1)}, bf16[1280,1024]{1,0:T(8,128)(2,1)}, u32[]{:S(2)}) copy-start(bf16[1280,1024]{1,0:T(8,128)(2,1)} %param.12) | copy-start | bytes 7864324
  7.2 63.1 %all-gather.12.cloned.1.call-start = ((), (), s32[]{:S(2)}) async-start(), calls=%async_computation.10 | async-start | bytes 2785280 | tf_op jit(solution)/shard_map/all_gather | solution.py:70
  7.9 113.1 %all-gather.10.cloned.1.call-start = ((), (), s32[]{:S(2)}) async-start(), calls=%async_computation.9 | async-start | bytes 2785280 | tf_op jit(solution)/shard_map/all_gather | solution.py:69
  11.0 50.2 %all-to-all-start.1 = ((bf16[4,1024,128]{2,1,0:T(8,128)(2,1)}), bf16[4,1024,128]{2,1,0:T(8,128)(2,1)}, u32[]{:S(2)}, u32[]{:S(2)}) async-start(bf16[4,1024,128]{2,1,0:T(8,128)(2,1)} %bitcast.122), calls=%async_computation.1 | async-start | bytes 2097152 | tf_op jit(solution)/shard_map/all_to_all | solution.py:82
  17.3 148.0 %all-gather.8.cloned.1.call-start = ((), (), s32[]{:S(2)}) async-start(), calls=%async_computation.8 | async-start | bytes 2785280 | tf_op jit(solution)/shard_map/all_gather | solution.py:71
  20.1 7.1 %collective-permute-start = (bf16[3,64,256]{2,1,0:T(8,128)(2,1)S(1)}, bf16[3,64,256]{2,1,0:T(8,128)(2,1)}, u32[]{:S(2)}, u32[]{:S(2)}) collective-permute-start(bf16[3,64,256]{2,1,0:T(8,128)(2,1)S(1)} %pad_maximum_fusion.2), channel_id=1, source_target_pairs={{4,0},{0,4},{5,1},{1,5},{6,2},{2,6},{7,3},{3,7},{12,8},{8,12},{13,... | collective-permute-start | bytes 294920 | tf_op jit(solution)/shard_map/ppermute | solution.py:11
  61.2 65.9 %all-to-all-start = ((bf16[128,4,1024]{2,0,1:T(8,128)(2,1)}), bf16[128,4,1024]{2,0,1:T(8,128)(2,1)}, u32[]{:S(2)}, u32[]{:S(2)}) async-start(bf16[128,4,1024]{2,0,1:T(8,128)(2,1)} %copy.21), calls=%async_computation | async-start | bytes 2097152 | tf_op jit(solution)/shard_map/all_to_all | solution.py:80
  67.3 250.5 %reduce-scatter.5.cloned.1.call-start = ((), (), s32[]{:S(2)}) async-start(), calls=%async_computation.7 | async-start | bytes 3063808 | tf_op jit(solution)/shard_map/reduce_scatter | solution.py:99
  79.0 92.4 %collective-permute-start.5 = (bf16[4,256,1024]{2,1,0:T(8,128)(2,1)}, bf16[4,256,1024]{2,1,0:T(8,128)(2,1)}, u32[]{:S(2)}, u32[]{:S(2)}) collective-permute-start(bf16[4,256,1024]{2,1,0:T(8,128)(2,1)} %add_convert_fusion), channel_id=1, source_target_pairs={{4,0},{0,4},{5,1},{1,5},{6,2},{2,6},{7,3},{3,7},{12,8},{8,12},{13,... | collective-permute-start | bytes 6291464 | tf_op jit(solution)/shard_map/ppermute | solution.py:11
  131.8 48.1 %collective-permute-start.2 = (bf16[4,256,1024]{2,1,0:T(8,128)(2,1)}, bf16[4,256,1024]{2,1,0:T(8,128)(2,1)}, u32[]{:S(2)}, u32[]{:S(2)}) collective-permute-start(bf16[4,256,1024]{2,1,0:T(8,128)(2,1)} %add_convert_fusion.1), channel_id=1, source_target_pairs={{4,0},{0,4},{5,1},{1,5},{6,2},{2,6},{7,3},{3,7},{12,8},{8,12},{13,... | collective-permute-start | bytes 6291464 | tf_op jit(solution)/shard_map/ppermute | solution.py:11
  196.7 47.1 %collective-permute-start.1 = (bf16[4,256,1024]{2,1,0:T(8,128)(2,1)S(1)}, bf16[4,256,1024]{2,1,0:T(8,128)(2,1)}, u32[]{:S(2)}, u32[]{:S(2)}) collective-permute-start(bf16[4,256,1024]{2,1,0:T(8,128)(2,1)S(1)} %add_convert_fusion.2), channel_id=1, source_target_pairs={{4,0},{0,4},{5,1},{1,5},{6,2},{2,6},{7,3},{3,7},{12,8},{8,12},{13,... | collective-permute-start | bytes 6291464 | tf_op jit(solution)/shard_map/ppermute | solution.py:11
  199.7 51.4 %all-to-all-start.2 = ((bf16[4,128,1024]{2,1,0:T(8,128)(2,1)}), bf16[4,128,1024]{2,1,0:T(8,128)(2,1)}, u32[]{:S(2)}, u32[]{:S(2)}) async-start(bf16[4,128,1024]{2,1,0:T(8,128)(2,1)} %convolution_convert_fusion.5), calls=%async_computation.4 | async-start | bytes 2097152 | tf_op jit(solution)/shard_map/all_to_all | solution.py:119
  209.9 38.2 %copy-start.18 = (bf16[1024,1280]{1,0:T(8,128)(2,1)S(1)}, bf16[1024,1280]{1,0:T(8,128)(2,1)}, u32[]{:S(2)}) copy-start(bf16[1024,1280]{1,0:T(8,128)(2,1)} %param.13) | copy-start | bytes 7864324
  251.2 29.0 %all-to-all-start.3 = ((bf16[4,1024,128]{2,1,0:T(8,128)(2,1)}), bf16[4,1024,128]{2,1,0:T(8,128)(2,1)}, u32[]{:S(2)}, u32[]{:S(2)}) async-start(bf16[4,1024,128]{2,1,0:T(8,128)(2,1)} %convolution_convert_fusion.4), calls=%async_computation.5 | async-start | bytes 2097152 | tf_op jit(solution)/shard_map/all_to_all | solution.py:116
  255.4 84.6 %reduce-scatter.3.cloned.1.call-start = ((), (), s32[]{:S(2)}) async-start(), calls=%async_computation.6 | async-start | bytes 3342336 | tf_op jit(solution)/shard_map/reduce_scatter | solution.py:109
  260.0 21.7 %copy-start.3 = (bf16[4,256,1024]{2,1,0:T(8,128)(2,1)S(1)}, bf16[4,256,1024]{2,1,0:T(8,128)(2,1)}, u32[]{:S(2)}) copy-start(bf16[4,256,1024]{2,1,0:T(8,128)(2,1)} %get-tuple-element.25) | copy-start | bytes 6291460
  269.2 29.4 %collective-permute-start.8 = (bf16[128,4096]{0,1:T(8,128)(2,1)}, bf16[128,4096]{0,1:T(8,128)(2,1)}, u32[]{:S(2)}, u32[]{:S(2)}) collective-permute-start(bf16[128,4096]{0,1:T(8,128)(2,1)} %bitcast.123), channel_id=1, source_target_pairs={{4,0},{0,4},{5,1},{1,5},{6,2},{2,6},{7,3},{3,7},{12,8},{8,12},{13,... | collective-permute-start | bytes 3145736 | tf_op jit(solution)/shard_map/ppermute | solution.py:11
  280.2 35.3 %collective-permute-start.9 = (bf16[4096,128]{1,0:T(8,128)(2,1)}, bf16[4096,128]{1,0:T(8,128)(2,1)}, u32[]{:S(2)}, u32[]{:S(2)}) collective-permute-start(bf16[4096,128]{1,0:T(8,128)(2,1)} %bitcast.36), channel_id=1, source_target_pairs={{4,0},{0,4},{5,1},{1,5},{6,2},{2,6},{7,3},{3,7},{12,8},{8,12},{13,... | collective-permute-start | bytes 3145736 | tf_op jit(solution)/shard_map/ppermute | solution.py:11
  318.5 9.6 %collective-permute-start.6 = (bf16[64,128]{1,0:T(8,128)(2,1)S(1)}, bf16[64,128]{1,0:T(8,128)(2,1)S(1)}, u32[]{:S(2)}, u32[]{:S(2)}) collective-permute-start(bf16[64,128]{1,0:T(8,128)(2,1)S(1)} %get-tuple-element.29), channel_id=1, source_target_pairs={{4,0},{0,4},{5,1},{1,5},{6,2},{2,6},{7,3},{3,7},{12,8},{8,12},{13,... | collective-permute-start | bytes 49160 | tf_op jit(solution)/shard_map/ppermute | solution.py:11
  328.1 16.7 %copy-start.14 = (bf16[1,64,1280]{2,1,0:T(8,128)(2,1)S(1)}, bf16[1,64,1280]{2,1,0:T(8,128)(2,1)}, u32[]{:S(2)}) copy-start(bf16[1,64,1280]{2,1,0:T(8,128)(2,1)} %param.9) | copy-start | bytes 491524
  328.5 11.6 %collective-permute-start.7 = (bf16[1,64,1280]{2,1,0:T(8,128)(2,1)S(1)}, bf16[1,64,1280]{2,1,0:T(8,128)(2,1)}, u32[]{:S(2)}, u32[]{:S(2)}) collective-permute-start(bf16[1,64,1280]{2,1,0:T(8,128)(2,1)S(1)} %fusion.11), channel_id=1, source_target_pairs={{8,0},{16,8},{24,16},{0,24},{9,1},{17,9},{25,17},{1,25},{10,2},{18... | collective-permute-start | bytes 491528 | tf_op jit(solution)/shard_map/ppermute | solution.py:11
  337.4 18.9 %copy-start.1 = (bf16[1280,1024]{1,0:T(8,128)(2,1)S(1)}, bf16[1280,1024]{1,0:T(8,128)(2,1)}, u32[]{:S(2)}) copy-start(bf16[1280,1024]{1,0:T(8,128)(2,1)} %param.12) | copy-start | bytes 7864324
  340.8 3.9 %collective-permute-start.3 = (bf16[64,2,128]{2,0,1:T(8,128)(2,1)S(1)}, bf16[64,2,128]{2,0,1:T(8,128)(2,1)S(1)}, u32[]{:S(2)}, u32[]{:S(2)}) collective-permute-start(bf16[64,2,128]{2,0,1:T(8,128)(2,1)S(1)} %copy_bitcast_fusion), channel_id=1, source_target_pairs={{4,0},{0,4},{5,1},{1,5},{6,2},{2,6},{7,3},{3,7},{12,8},{8,12},{13,... | collective-permute-start | bytes 98312 | tf_op jit(solution)/shard_map/ppermute | solution.py:11
  346.0 8.0 %collective-permute-start.4 = (bf16[1,64,1280]{2,1,0:T(8,128)(2,1)S(1)}, bf16[1,64,1280]{2,1,0:T(8,128)(2,1)S(1)}, u32[]{:S(2)}, u32[]{:S(2)}) collective-permute-start(bf16[1,64,1280]{2,1,0:T(8,128)(2,1)S(1)} %fusion.12), channel_id=1, source_target_pairs={{24,0},{0,8},{8,16},{16,24},{25,1},{1,9},{9,17},{17,25},{26,2},{2,... | collective-permute-start | bytes 491528 | tf_op jit(solution)/shard_map/ppermute | solution.py:11
  (14 other events, 62.1 us)
Sparse Core Ops, SparseCore 0:
  10.3 59.9 all-gather.11
  72.6 48.3 all-gather.9
  123.3 41.9 all-gather.7
  192.6 65.6 reduce-scatter.4
  262.4 65.3 reduce-scatter.2
where the time goes:
time: 364 us; the launch traced here: 363 us
  waiting for transfers between devices  147 us (40%)
  matrix products  68.5 us (19%)
  blocking collectives  43.2 us (12%)
  starting transfers between devices  35.8 us (10%)
  local copies, waits for them, and re-layouts  34.7 us (10%)
  other arithmetic  19.6 us (5%)
  between operations  14.1 us (4%)
    dot_general x21, matrix products, mm(): return jnp.einsum(spec, left, right, preferred_element_type=F32)  68.5 us
    ppermute x10, waiting for transfers between devices, from_behind(): lax.ppermute(block, axis, [((i - distance) % count, i) for i in range(cou...  59.8 us
    all_gather x1, waiting for transfers between devices, local(): all_bwd = lax.all_gather(x_bwd, everyone, axis=0, tiled=True)  40.5 us
    all_gather x1, blocking collectives, local(): low_all = lax.all_gather(low, everyone, axis=1, tiled=True)  32.3 us
    all_gather x1, waiting for transfers between devices, local(): all_fwd = lax.all_gather(x_fwd, everyone, axis=0, tiled=True)  32 us
    ppermute x10, starting transfers between devices, from_behind(): lax.ppermute(block, axis, [((i - distance) % count, i) for i in range(cou...  14.5 us
    unnamed x42, local copies, waits for them, and re-layouts  12.3 us
    all_to_all x1, waiting for transfers between devices, local(): grad_left = lax.all_to_all(grad_left, 'section', 0, 0, tiled=True)  9.54 us
  transfers between devices with their start and end apart: 19, of which 8 were waited for; matrix products, arithmetic and copies ran while one was open for 28% of the time, Pallas kernels for 0%

commit v1 on v0

--- a/solution.py
+++ b/solution.py
@@ -1,6 +1,11 @@
+import functools
+import types
+
 import jax
 import jax.numpy as jnp
 from jax import lax
+from jax.experimental import pallas as pl
+from jax.experimental.pallas import tpu as pltpu
 from jax.sharding import PartitionSpec as P
 
 F32, BF16 = jnp.float32, jnp.bfloat16
@@ -142,6 +147,754 @@
         grad_down_left[None],
         grad_down_right[None],
     )
+
+
+MESH = pl.DeviceIdType.MESH
+SECTION, ROW, COL = "section", "row", "col"
+BWD, COT, FWD, LOW = range(4)
+TILE = 256
+FULL = 1
+VMEM_BYTES = 63 * 1024 * 1024
+
+
+def nn(left, right):
+    return lax.dot_general(left, right, (((1,), (0,)), ((), ())), preferred_element_type=F32)
+
+
+def nt(left, right):
+    return lax.dot_general(left, right, (((1,), (1,)), ((), ())), preferred_element_type=F32)
+
+
+def tn(left, right):
+    return lax.dot_general(left, right, (((0,), (0,)), ((), ())), preferred_element_type=F32)
+
+
+def at(index, size):
+    return pl.ds(pl.multiple_of(index * size, size), size)
+
+
+def scratch_of(S, C, own, width, units, rank):
+    share, micro = rank // 2, own * C
+    wide_b, wide_f = width + 2 * share, width + share
+    arrays = dict(
+        tok=(3, S, C, own, width),
+        low=(S, C, 5, own, share),
+        low_part=(3, own, rank),
+        low_in=(3, own, rank),
+        rt=(S, share, units),
+        lt=(S, units, share),
+        wu=(width, units),
+        wd=(units, width),
+        ul=(width, rank),
+        dr=(rank, width),
+        mine=(3, S, micro, units),
+        theirs=(3, S, micro, units),
+        rs_b=(S, 2, C // 2, own, wide_b),
+        rk_b=(S, C // 2, own, wide_b),
+        ry_b=(S, C // 2, own, wide_b),
+        rs_f=(S, 2, C // 2, own, wide_f),
+        rk_f=(S, C // 2, own, wide_f),
+        ry_f=(S, C // 2, own, wide_f),
+        zs_b=(S, own, wide_b),
+        zr_b=(S, own, wide_b),
+        zs_f=(S, own, wide_f),
+        zr_f=(S, own, wide_f),
+        gl_out=(S, 2, units, share),
+        gr_out=(S, 2, share, units),
+        gl_in=(2, S, units, share),
+        gr_in=(2, S, share, units),
+        gu_tile=(2, TILE, units),
+        gd_tile=(2, TILE, width),
+        rank_out=(3, own, share),
+        rank_in=(3, own, share),
+        rank_all=(C, 2, own, rank),
+        hand=(2, own, width),
+    )
+    shapes = {name: pltpu.VMEM(shape, BF16) for name, shape in arrays.items()}
+    shapes["gul"] = pltpu.VMEM((width, rank), F32)
+    shapes["gdr"] = pltpu.VMEM((rank, width), F32)
+    sems = dict(
+        s_load=(12,),
+        s_put=(6,),
+        s_gput=(2, 2, S),
+        s_gu_put=(2,),
+        s_gd_put=(2,),
+        s_tz=(2, 4, S),
+        s_ty=(2, 4, S, C // 2),
+        s_tk=(2, 4, S, C // 2),
+        s_fac=(2, 2, S),
+        s_low_x=(2,),
+        s_pre=(2, 3, S),
+        s_rk=(2, 2, S),
+        s_ry=(2, 2, S, C // 2),
+        s_rz=(2, 2, S),
+        s_gz=(2, 4, S),
+        s_gx=(2, 2, S),
+        s_rank_x=(2, 2),
+        s_rank_c=(2, C),
+        s_hand_z=(2, 2),
+    )
+    for name, shape in sems.items():
+        shapes[name] = pltpu.SemaphoreType.DMA(shape)
+    return shapes
+
+
+def vmem_need(shapes):
+    total = 0
+    for name, ref in shapes.items():
+        if not name.startswith("s_"):
+            size = jnp.dtype(ref.dtype).itemsize
+            for extent in ref.shape:
+                size *= extent
+            total += size
+    return total
+
+
+def kernel(S, C, names, *refs):
+    xf_h, xb_h, ct_h, wu_h, wd_h, ul_h, ur_h, dl_h, dr_h = refs[:9]
+    hf_o, hb_o, gu_o, gd_o, gul_o, gl_o, gr_o, gdr_o = refs[9:17]
+    v = types.SimpleNamespace(**dict(zip(names, refs[17:])))
+    tok, low, rt, lt, mine, theirs = v.tok, v.low, v.rt, v.lt, v.mine, v.theirs
+    wu, wd, ul, dr = v.wu, v.wd, v.ul, v.dr
+    own, width = tok.shape[3], tok.shape[4]
+    units, share = lt.shape[1], lt.shape[2]
+    rank, micro, Y = 2 * share, own * C, C // 2
+    z, r, c = (lax.axis_index(axis) for axis in (SECTION, ROW, COL))
+    y, core = c // 2, lax.rem(c, 2)
+    my_half, other_half = at(r, share), at(1 - r, share)
+
+    def behind(d):
+        return lax.rem(z - d + S, S)
+
+    def ahead(d):
+        return lax.rem(z + d, S)
+
+    def col_up(e):
+        return lax.rem(c + e, C)
+
+    def col_down(e):
+        return lax.rem(c - e + C, C)
+
+    def y_up(g):
+        return lax.rem(y + g, Y)
+
+    def y_down(g):
+        return lax.rem(y - g + Y, Y)
+
+    def remote(source, target, sem, index, where):
+        return pltpu.make_async_remote_copy(
+            src_ref=source,
+            dst_ref=target,
+            send_sem=sem.at[(0,) + index],
+            recv_sem=sem.at[(1,) + index],
+            device_id=where,
+            device_id_type=MESH,
+        )
+
+    def piece(t, s, col):
+        return low.at[s, col] if t == LOW else tok.at[t, s, col]
+
+    def tok_z(t, d):
+        return remote(piece(t, z, c), piece(t, z, c), v.s_tz, (t, d), {SECTION: ahead(d)})
+
+    def tok_z_in(t, d):
+        here = piece(t, behind(d), c)
+        return remote(here, here, v.s_tz, (t, d), {SECTION: ahead(d)})
+
+    def tok_y(t, d, g):
+        here = piece(t, behind(d), c)
+        return remote(here, here, v.s_ty, (t, d, g), {COL: 2 * y_up(g) + core})
+
+    def tok_y_in(t, d, g):
+        here = piece(t, behind(d), 2 * y_down(g) + core)
+        return remote(here, here, v.s_ty, (t, d, g), {COL: 2 * y_up(g) + core})
+
+    def tok_k(t, d, g):
+        here = piece(t, behind(d), 2 * y_down(g) + core)
+        return remote(here, here, v.s_tk, (t, d, g), {COL: 2 * y + 1 - core})
+
+    def tok_k_in(t, d, g):
+        here = piece(t, behind(d), 2 * y_down(g) + 1 - core)
+        return remote(here, here, v.s_tk, (t, d, g), {COL: 2 * y + 1 - core})
+
+    def fac(k, d):
+        if k == 0:
+            return remote(ur_h.at[my_half, at(ahead(d), units)], rt.at[z], v.s_fac, (0, d), {SECTION: ahead(d)})
+        return remote(dl_h.at[at(ahead(d), units), my_half], lt.at[z], v.s_fac, (1, d), {SECTION: ahead(d)})
+
+    def fac_in(k, d):
+        here = (rt if k == 0 else lt).at[behind(d)]
+        return remote(here, here, v.s_fac, (k, d), {SECTION: ahead(d)})
+
+    def low_x():
+        return remote(v.low_part, v.low_in, v.s_low_x, (), {ROW: 1 - r})
+
+    def pre(j, d):
+        s = behind(d)
+        return remote(mine.at[j, s], theirs.at[j, s], v.s_pre, (j, d), {ROW: 1 - r})
+
+    def sums(j):
+        return (v.rs_b, v.rk_b, v.ry_b, v.zs_b, v.zr_b) if j == 0 else (v.rs_f, v.rk_f, v.ry_f, v.zs_f, v.zr_f)
+
+    def rs_k(j, d):
+        rs, rk = sums(j)[:2]
+        return remote(rs.at[behind(d), 1 - core], rk.at[behind(d)], v.s_rk, (j, d), {COL: 2 * y + 1 - core})
+
+    def rs_y(j, d, g):
+        rs, _, ry, _, _ = sums(j)
+        s = behind(d)
+        return remote(rs.at[s, core, y_up(g)], ry.at[s, y], v.s_ry, (j, d, g), {COL: 2 * y_up(g) + core})
+
+    def rs_y_in(j, d, g):
+        here = sums(j)[2].at[behind(d), y_down(g)]
+        return remote(here, here, v.s_ry, (j, d, g), {COL: 2 * y_up(g) + core})
+
+    def rs_z(j, d):
+        zs, zr = sums(j)[3:]
+        return remote(zs.at[behind(d)], zr.at[z], v.s_rz, (j, d), {SECTION: behind(d)})
+
+    def rs_z_in(j, d):
+        here = sums(j)[4].at[ahead(d)]
+        return remote(here, here, v.s_rz, (j, d), {SECTION: behind(d)})
+
+    def grad_slot(k, s, half):
+        return (v.gl_in if k == 0 else v.gr_in).at[half, s]
+
+    def grad_source(k, s, other):
+        return (v.gl_out if k == 0 else v.gr_out).at[s, other]
+
+    def halves(other):
+        return 1 - r if other else r
+
+    def grad_z(k, d, other=0):
+        slot = grad_slot(k, z, halves(other))
+        return remote(grad_source(k, behind(d), other), slot, v.s_gz, (2 * other + k, d), {SECTION: behind(d)})
+
+    def grad_z_in(k, d, other=0):
+        here = grad_slot(k, ahead(d), halves(other))
+        return remote(here, here, v.s_gz, (2 * other + k, d), {SECTION: behind(d)})
+
+    def grad_keep(k, other):
+        source = grad_source(k, z, other)
+        half = other_half if other else my_half
+        target = gl_o.at[at(z, units), half] if k == 0 else gr_o.at[half, at(z, units)]
+        return pltpu.make_async_copy(source, target, v.s_put.at[2 * other + k])
+
+    def grad_put(k, d, half):
+        s, lanes = ahead(d), pl.ds(half * share, share)
+        target = gl_o.at[at(s, units), lanes] if k == 0 else gr_o.at[lanes, at(s, units)]
+        return pltpu.make_async_copy(grad_slot(k, s, half), target, v.s_gput.at[k, half, d])
+
+    def grad_x(k, d):
+        here = grad_slot(k, ahead(d), r)
+        return remote(here, here, v.s_gx, (k, d), {ROW: 1 - r})
+
+    def grad_x_in(k, d):
+        here = grad_slot(k, ahead(d), 1 - r)
+        return remote(here, here, v.s_gx, (k, d), {ROW: 1 - r})
+
+    def rank_x(j):
+        block = pl.ds(0, 2) if j == 0 else pl.ds(2, 1)
+        return remote(v.rank_out.at[block], v.rank_in.at[block], v.s_rank_x, (j,), {ROW: 1 - r})
+
+    def rank_c(e):
+        here = v.rank_all.at[c]
+        return remote(here, here, v.s_rank_c, (e,), {COL: col_up(e)})
+
+    def rank_c_in(e):
+        here = v.rank_all.at[col_down(e)]
+        return remote(here, here, v.s_rank_c, (e,), {COL: col_up(e)})
+
+    def hand(j):
+        if j == 0:
+            return remote(v.hand.at[0], hb_o, v.s_hand_z, (0,), {SECTION: behind(1)})
+        return remote(v.hand.at[1], hf_o, v.s_hand_z, (1,), {SECTION: ahead(1)})
+
+    def spread(t, d):
+        for g in range(1, Y):
+            tok_y(t, d, g).start()
+        tok_k(t, d, 0).start()
+
+    def forward(t, d):
+        tok_z_in(t, d).wait_recv()
+        spread(t, d)
+
+    def send(d):
+        for t in (BWD, COT):
+            tok_z(t, d).start()
+        for k in range(2):
+            fac(k, d).start()
+        tok_z(FWD, d).start()
+
+    def gathered(t, d):
+        for g in range(1, Y):
+            tok_y_in(t, d, g).wait_recv()
+            tok_k(t, d, g).start()
+        for g in range(Y):
+            tok_k_in(t, d, g).wait_recv()
+
+    def tokens(t, s):
+        return tok[t, s].reshape(micro, width)
+
+    def rank_tokens(t, s, half=r):
+        return low[s, :, 4 if t == FWD else 2 * t + half].reshape(micro, share)
+
+    def partial_up(j, t, d):
+        s = behind(d)
+
+        @pl.loop(0, units // min(TILE, units))
+        def _(n):
+            cols = at(n, min(TILE, units))
+            part = nn(tokens(t, s), wu[:, cols]) + nn(rank_tokens(t, s), rt[s, :, cols])
+            mine[j, s, :, cols] = part.astype(BF16)
+
+        pre(j, d).start()
+
+    def partial_down(d):
+        s = behind(d)
+
+        @pl.loop(0, units // min(TILE, units))
+        def _(n):
+            cols = at(n, min(TILE, units))
+            part = nt(tokens(COT, s), wd[cols, :]) + nt(rank_tokens(COT, s), lt[s, cols, :])
+            mine[1, s, :, cols] = part.astype(BF16)
+
+        pre(1, d).start()
+
+    def bwd_partials(d, first):
+        gathered(BWD, d)
+        gathered(LOW, d)
+        if not first:
+            fac_in(0, d).wait_recv()
+        partial_up(0, BWD, d)
+        gathered(COT, d)
+        if not first:
+            fac_in(1, d).wait_recv()
+        partial_down(d)
+
+    def fwd_partials(d):
+        gathered(FWD, d)
+        partial_up(2, FWD, d)
+
+    def by_owner(rs, s, cols, part):
+        part = part.astype(BF16)
+        for col in range(C):
+            rs[s, col % 2, col // 2, :, cols] = part[col * own : (col + 1) * own]
+
+    def bwd_chunk(d):
+        s = behind(d)
+        for j in range(2):
+            pre(j, d).wait()
+
+        @pl.loop(0, units // min(TILE, units))
+        def _(n):
+            cols = at(n, min(TILE, units))
+            p = mine[0, s, :, cols].astype(F32) + theirs[0, s, :, cols].astype(F32)
+            g = mine[1, s, :, cols].astype(F32) + theirs[1, s, :, cols].astype(F32)
+            sigma = jax.nn.sigmoid(p)
+            mine[0, s, :, cols] = (p * sigma).astype(BF16)
+            mine[1, s, :, cols] = (g * (sigma * (1.0 + p * (1.0 - sigma)))).astype(BF16)
+
+        @pl.loop(0, width // TILE)
+        def _(n):
+            cols = at(n, TILE)
+            by_owner(v.rs_b, s, cols, nt(mine[1, s], wu[cols, :]))
+
+        by_owner(v.rs_b, s, slice(width, width + share), nt(mine[1, s], rt[s]))
+        by_owner(v.rs_b, s, slice(width + share, width + 2 * share), nn(mine[0, s], lt[s]))
+        rs_k(0, d).start()
+        v.gl_out[s, 0] = tn(mine[0, s], rank_tokens(COT, s)).astype(BF16)
+        v.gr_out[s, 0] = tn(rank_tokens(BWD, s), mine[1, s]).astype(BF16)
+
+        @pl.when(d > 0)
+        def _():
+            for k in range(2):
+                grad_z(k, d).start()
+
+        @pl.when(d < FULL)
+        def _():
+            v.gl_out[s, 1] = tn(mine[0, s], rank_tokens(COT, s, 1 - r)).astype(BF16)
+            v.gr_out[s, 1] = tn(rank_tokens(BWD, s, 1 - r), mine[1, s]).astype(BF16)
+
+        @pl.when((d < FULL) & (d > 0))
+        def _():
+            for k in range(2):
+                grad_z(k, d, 1).start()
+
+        @pl.when(d == 0)
+        def _():
+            for k in range(2):
+                for other in range(2):
+                    grad_keep(k, other).start()
+
+    def fwd_chunk(d):
+        s = behind(d)
+        pre(2, d).wait()
+
+        @pl.loop(0, units // min(TILE, units))
+        def _(n):
+            cols = at(n, min(TILE, units))
+            p = mine[2, s, :, cols].astype(F32) + theirs[2, s, :, cols].astype(F32)
+            mine[2, s, :, cols] = (p * jax.nn.sigmoid(p)).astype(BF16)
+
+        @pl.loop(0, width // TILE)
+        def _(n):
+            cols = at(n, TILE)
+            by_owner(v.rs_f, s, cols, nn(mine[2, s], wd[:, cols]))
+
+        by_owner(v.rs_f, s, slice(width, width + share), nn(mine[2, s], lt[s]))
+        rs_k(1, d).start()
+
+    def reduce_core(j, d):
+        s = behind(d)
+        rs, rk = sums(j)[:2]
+        rs_k(j, d).wait()
+        rs[s, core] = (rs[s, core].astype(F32) + rk[s].astype(F32)).astype(BF16)
+        for g in range(1, Y):
+            rs_y(j, d, g).start()
+
+    def reduce_chunk(j, d):
+        s = behind(d)
+        rs, _, ry, zs, zr = sums(j)
+        total = rs[s, core, y].astype(F32)
+        for g in range(1, Y):
+            rs_y_in(j, d, g).wait_recv()
+            total = total + ry[s, y_down(g)].astype(F32)
+
+        @pl.when(d == 0)
+        def _():
+            zr[z] = total.astype(BF16)
+
+        @pl.when(d > 0)
+        def _():
+            zs[s] = total.astype(BF16)
+            rs_z(j, d).start()
+
+    def pass_on(d):
+        for k in range(2):
+            grad_z_in(k, d).wait_recv()
+            grad_x(k, d).start()
+
+    def home_sum(j):
+        zr = sums(j)[4]
+        for d in range(1, S):
+            rs_z_in(j, d).wait_recv()
+        total = zr[0].astype(F32)
+        for s in range(1, S):
+            total = total + zr[s].astype(F32)
+        return total
+
+    def grad_up():
+        step = min(TILE, units)
+
+        @pl.loop(0, width // TILE)
+        def _(m):
+            slot = lax.rem(m, 2)
+            put = pltpu.make_async_copy(v.gu_tile.at[slot], gu_o.at[at(m, TILE), :], v.s_gu_put.at[slot])
+
+            @pl.when(m >= 2)
+            def _():
+                put.wait()
+
+            for n in range(units // step):
+                left = tok[BWD, :, :, :, at(m, TILE)].reshape(S * micro, TILE)
+                right = mine[1, :, :, n * step : (n + 1) * step].reshape(S * micro, step)
+                v.gu_tile[slot, :, n * step : (n + 1) * step] = tn(left, right).astype(BF16)
+            put.start()
+
+    def grad_down():
+        tall = min(TILE, units)
+
+        @pl.loop(0, units // tall)
+        def _(m):
+            slot = lax.rem(m, 2)
+            put = pltpu.make_async_copy(
+                v.gd_tile.at[slot, :tall], gd_o.at[at(m, tall), :], v.s_gd_put.at[slot]
+            )
+
+            @pl.when(m >= 2)
+            def _():
+                put.wait()
+
+            for n in range(width // TILE):
+                left = mine[0, :, :, at(m, tall)].reshape(S * micro, tall)
+                right = tok[COT, :, :, :, n * TILE : (n + 1) * TILE].reshape(S * micro, TILE)
+                v.gd_tile[slot, :tall, n * TILE : (n + 1) * TILE] = tn(left, right).astype(BF16)
+            put.start()
+
+    def drain_tiles(sem, tile, out, tall, count):
+        for m in range(max(0, count - 2), count):
+            pltpu.make_async_copy(
+                tile.at[m % 2, :tall], out.at[m * tall : (m + 1) * tall, :], sem.at[m % 2]
+            ).wait()
+
+    loads = [
+        (xb_h, tok.at[BWD, z, c]),
+        (ct_h, tok.at[COT, z, c]),
+        (xf_h, tok.at[FWD, z, c]),
+        (ul_h, ul),
+        (dr_h, dr),
+        (wu_h, wu),
+        (ur_h.at[my_half, at(z, units)], rt.at[z]),
+        (wd_h, wd),
+        (dl_h.at[at(z, units), my_half], lt.at[z]),
+    ]
+    loads = [pltpu.make_async_copy(a, b, v.s_load.at[i]) for i, (a, b) in enumerate(loads)]
+    for copy in loads:
+        copy.start()
+    barrier = pltpu.get_barrier_semaphore()
+    pl.semaphore_signal(barrier, inc=1, device_id={ROW: 1 - r}, device_id_type=MESH)
+    for e in range(1, C):
+        pl.semaphore_signal(barrier, inc=1, device_id={COL: col_up(e)}, device_id_type=MESH)
+    for d in range(1, S):
+        pl.semaphore_signal(barrier, inc=1, device_id={SECTION: ahead(d)}, device_id_type=MESH)
+    for copy in loads[:3]:
+        copy.wait()
+    pl.semaphore_wait(barrier, S + C - 1)
+
+    spread(BWD, 0)
+    spread(COT, 0)
+    send(1)
+    for copy in loads[3:5]:
+        copy.wait()
+    v.low_part[BWD] = nn(tok[BWD, z, c], ul[...]).astype(BF16)
+    v.low_part[COT] = nt(tok[COT, z, c], dr[...]).astype(BF16)
+    v.low_part[FWD] = nn(tok[FWD, z, c], ul[...]).astype(BF16)
+    low_x().start()
+    low_x().wait()
+    for t in (BWD, COT):
+        for half in range(2):
+            cols = pl.ds(half * share, share)
+            low[z, c, 2 * t + half] = (v.low_part[t, :, cols].astype(F32) + v.low_in[t, :, cols].astype(F32)).astype(BF16)
+    low[z, c, 4] = (v.low_part[FWD, :, my_half].astype(F32) + v.low_in[FWD, :, my_half].astype(F32)).astype(BF16)
+    spread(LOW, 0)
+    for d in range(1, S):
+        tok_z(LOW, d).start()
+    spread(FWD, 0)
+    for copy in loads[5:]:
+        copy.wait()
+    bwd_partials(0, True)
+    fwd_partials(0)
+    for t in (BWD, LOW, COT, FWD):
+        forward(t, 1)
+    send(2)
+
+    @pl.loop(0, S)
+    def _(i):
+        @pl.when(i + 1 < S)
+        def _():
+            bwd_partials(i + 1, False)
+            fwd_partials(i + 1)
+
+        @pl.when(i > 0)
+        def _():
+            reduce_chunk(0, i - 1)
+            reduce_chunk(1, i - 1)
+
+        bwd_chunk(i)
+        reduce_core(0, i)
+        fwd_chunk(i)
+        reduce_core(1, i)
+
+        @pl.when(i + 2 < S)
+        def _():
+            for t in (BWD, LOW, COT, FWD):
+                forward(t, i + 2)
+
+        @pl.when(i + 3 < S)
+        def _():
+            send(i + 3)
+
+        @pl.when(i > FULL)
+        def _():
+            pass_on(i - 1)
+
+    reduce_chunk(0, S - 1)
+    reduce_chunk(1, S - 1)
+    grad_up()
+    if FULL < S:
+        pass_on(S - 1)
+
+    total = home_sum(0)
+    v.rank_out[0] = total[:, width : width + share].astype(BF16)
+    v.rank_out[1] = total[:, width + share :].astype(BF16)
+    rank_x(0).start()
+    grad_norm = total[:, :width] + tok[COT, z, c].astype(F32)
+    rank_x(0).wait()
+    v.rank_all[c, :, :, my_half] = v.rank_out[0:2]
+    v.rank_all[c, :, :, other_half] = v.rank_in[0:2]
+    for e in range(1, C):
+        rank_c(e).start()
+    v.hand[0] = (grad_norm + nt(v.rank_all[c, 0], ul[...])).astype(BF16)
+    hand(0).start()
+
+    grad_down()
+
+    total = home_sum(1)
+    v.rank_out[2] = total[:, width:].astype(BF16)
+    rank_x(1).start()
+    for e in range(1, C):
+        rank_c_in(e).wait_recv()
+    v.gul[...] = tn(tokens(BWD, z), v.rank_all[:, 0].reshape(micro, rank))
+    put_up = pltpu.make_async_copy(v.gul, gul_o, v.s_put.at[4])
+    put_up.start()
+    v.gdr[...] = tn(v.rank_all[:, 1].reshape(micro, rank), tokens(COT, z))
+    put_down = pltpu.make_async_copy(v.gdr, gdr_o, v.s_put.at[5])
+    put_down.start()
+    rank_x(1).wait()
+    out = total[:, :width] + tok[FWD, z, c].astype(F32)
+    out = out + nn(v.rank_out[2], dr[my_half, :]) + nn(v.rank_in[2], dr[other_half, :])
+    v.hand[1] = out.astype(BF16)
+    hand(1).start()
+
+    for k in range(2):
+        for other in range(2):
+            grad_keep(k, other).wait()
+        for d in range(1, FULL):
+            grad_z_in(k, d).wait_recv()
+            grad_z_in(k, d, 1).wait_recv()
+            grad_z(k, d, 1).wait_send()
+            for half in range(2):
+                grad_put(k, d, half).start()
+
+    @pl.loop(FULL, S)
+    def _(d):
+        for k in range(2):
+            grad_x(k, d).wait_send()
+            grad_x_in(k, d).wait_recv()
+            for half in range(2):
+                grad_put(k, d, half).start()
+
+    tall = min(TILE, units)
+    drain_tiles(v.s_gu_put, v.gu_tile, gu_o, TILE, width // TILE)
+    drain_tiles(v.s_gd_put, v.gd_tile, gd_o, tall, units // tall)
+    put_up.wait()
+    put_down.wait()
+
+    @pl.loop(1, S)
+    def _(d):
+        for t in range(4):
+            tok_z(t, d).wait_send()
+        for k in range(2):
+            fac(k, d).wait_send()
+            grad_z(k, d).wait_send()
+            rs_z(k, d).wait_send()
+
+    @pl.loop(0, S)
+    def _(d):
+        for t in range(4):
+            for g in range(Y):
+                tok_k(t, d, g).wait_send()
+            for g in range(1, Y):
+                tok_y(t, d, g).wait_send()
+        for j in range(2):
+            for g in range(1, Y):
+                rs_y(j, d, g).wait_send()
+
+    for e in range(1, C):
+        rank_c(e).wait_send()
+    for j in range(2):
+        hand(j).wait()
+
+    @pl.loop(1, S)
+    def _(d):
+        for k in range(2):
+            for half in range(2):
+                grad_put(k, d, half).wait()
+
+
+def finish_kernel(count, *refs):
+    ins, outs, near, wide = refs[:8], refs[8:16], refs[16:24], refs[24:26]
+    s_in, s_out = refs[26:]
+    pieces = []
+    for i in (5, 6, 2, 3, 4, 7, 0, 1):
+        parts = count if i in (2, 3, 5, 6) else 1
+        tall = ins[i].shape[0] // parts
+        for p in range(parts):
+            rows = pl.ds(p * tall, tall)
+            final = wide[i - 5] if i in (5, 6) else near[i]
+            load = pltpu.make_async_copy(ins[i].at[rows], near[i].at[rows], s_in.at[i, p])
+            store = pltpu.make_async_copy(final.at[rows], outs[i].at[rows], s_out.at[i, p])
+            pieces.append((i, rows, load, store))
+    for _, _, load, _ in pieces:
+        load.start()
+    for i, rows, load, store in pieces:
+        load.wait()
+        if i in (5, 6):
+            wide[i - 5][rows] = near[i][rows].astype(F32)
+        store.start()
+    for _, _, _, store in pieces:
+        store.wait()
+
+
+def finish(arrays):
+    whole, count = pl.BlockSpec(memory_space=pl.ANY), 4
+    outs = [jax.ShapeDtypeStruct(a.shape, F32 if i in (5, 6) else a.dtype) for i, a in enumerate(arrays)]
+    return pl.pallas_call(
+        functools.partial(finish_kernel, count),
+        out_shape=outs,
+        in_specs=[whole] * len(outs),
+        out_specs=[whole] * len(outs),
+        scratch_shapes=[pltpu.VMEM(a.shape, a.dtype) for a in arrays]
+        + [pltpu.VMEM(outs[i].shape, F32) for i in (5, 6)]
+        + [pltpu.SemaphoreType.DMA((8, count))] * 2,
+        compiler_params=pltpu.CompilerParams(vmem_limit_bytes=VMEM_BYTES),
+    )(*arrays)
+
+
+def fused(*args):
+    S, C = lax.axis_size(SECTION), lax.axis_size(COL)
+    own, width = args[0].shape[1:]
+    units, rank = args[3].shape[1], args[5].shape[2]
+    shapes = scratch_of(S, C, own, width, units, rank)
+    outs = [
+        ((own, width), BF16),
+        ((own, width), BF16),
+        ((width, units), BF16),
+        ((units, width), BF16),
+        ((width, rank), F32),
+        ((S * units, rank), BF16),
+        ((rank, S * units), BF16),
+        ((rank, width), F32),
+    ]
+    whole = pl.BlockSpec(memory_space=pl.ANY)
+    tokens = 3 * S * own * C
+    outputs = pl.pallas_call(
+        functools.partial(kernel, S, C, list(shapes)),
+        out_shape=[jax.ShapeDtypeStruct(*out) for out in outs],
+        in_specs=[whole] * len(args),
+        out_specs=[whole] * len(outs),
+        scratch_shapes=list(shapes.values()),
+        compiler_params=pltpu.CompilerParams(
+            collective_id=0, has_side_effects=True, vmem_limit_bytes=VMEM_BYTES
+        ),
+        cost_estimate=pl.CostEstimate(
+            flops=6 * tokens * width * units, bytes_accessed=20 * width * units, transcendentals=tokens * units
+        ),
+    )(*[arg[0] if arg.ndim == 3 else arg for arg in args])
+    hand_f, hand_b, grad_up, grad_down, grad_ul, grad_dl, grad_ur, grad_dr = finish(outputs)
+    return (
+        hand_f[None],
+        hand_b[None],
+        grad_up,
+        grad_down,
+        grad_ul[None],
+        grad_ur[None],
+        grad_dl[None],
+        grad_dr[None],
+    )
+
+
+def step(*args):
+    S, C, rows = (lax.axis_size(axis) for axis in (SECTION, COL, ROW))
+    own, width = args[0].shape[1:]
+    units, rank = args[3].shape[1], args[5].shape[2]
+    shapes = scratch_of(S, C, own, width, units, rank)
+    fits = vmem_need(shapes) <= VMEM_BYTES - (2 << 20)
+    even = rows == 2 and S > 2 and C % 2 == 0 and width % TILE == 0 and (units % TILE == 0 or units == 128)
+    if fits and even and rank == 256 and own % 16 == 0:
+        return fused(*args)
+    return local(*args)
 
 
 def solution(mesh):
@@ -166,4 +919,4 @@
         P("section", "col", None),
         P("section", None, "row"),
     )
-    return jax.shard_map(local, mesh=mesh, in_specs=in_specs, out_specs=out_specs, check_vma=False)
+    return jax.shard_map(step, mesh=mesh, in_specs=in_specs, out_specs=out_specs, check_vma=False)

time: 364 us -> 231 us (0.63)
  Pallas kernels: 0 us -> 231 us
  waiting for transfers between devices: 147 us -> 0 us
  matrix products: 68.5 us -> 0 us
  blocking collectives: 43.2 us -> 0 us
  starting transfers between devices: 35.8 us -> 0 us
  local copies, waits for them, and re-layouts: 34.7 us -> 0 us
  other arithmetic: 19.6 us -> 0 us
  between operations: 14.1 us -> 0.64 us
    pallas_call x0 -> x2, Pallas kernels: none -> 231 us  [the longest x1 220 us: fused(): pl.pallas_call(functools.partial(kernel, S, C, list(shapes)), out_shape=[...]
    all_gather x3 -> x0, waiting for transfers between devices: 75.5 us -> none  [the longest x1 40.5 us: local(): all_bwd = lax.all_gather(x_bwd, everyone, axis=0, tiled=True)]
    dot_general x21 -> x0, matrix products: 68.5 us -> none  [mm(): return jnp.einsum(spec, left, right, preferred_element_type=F32)]
    ppermute x10 -> x0, waiting for transfers between devices: 59.8 us -> none  [from_behind(): lax.ppermute(block, axis, [((i - distance) % count, i) for i in range(cou...]
    all_gather x3 -> x0, blocking collectives: 43.2 us -> none  [the longest x1 32.3 us: local(): low_all = lax.all_gather(low, everyone, axis=1, tiled=True)]
    all_to_all x4 -> x0, starting transfers between devices: 21.1 us -> none  [the longest x1 6.32 us: local(): lax.all_to_all(own_share(down_left[0], 0 + 1), 'section', 0, 0, tiled=True)]
    ppermute x10 -> x0, starting transfers between devices: 14.5 us -> none  [from_behind(): lax.ppermute(block, axis, [((i - distance) % count, i) for i in range(cou...]
    unnamed x42 -> x0, local copies, waits for them, and re-layouts: 12.3 us -> none
  transfers between devices with their start and end apart: 19 -> 0, of which waited for: 8 -> 0; matrix products, arithmetic and copies ran while one was open for 28% -> 0% of each run, Pallas kernels for 0% -> 0%
where the time goes in v1:
time: 231 us
  Pallas kernels  231 us (100%)
    pallas_call x1, Pallas kernels, fused(): pl.pallas_call(functools.partial(kernel, S, C, list(shapes)), out_shape=[...  220 us
    pallas_call x1, Pallas kernels, finish(): pl.pallas_call(functools.partial(finish_kernel, count), out_shape=outs, i...  10.9 us

profile of v1, /device:TPU:0, one launch (start us, length us, event | category | flops | bytes accessed | tf_op | source)
XLA Modules:
  0.0 231.3 jit_solution(16582091835018727218)
XLA Ops:
  0.6 219.8 %shard_map.152 = (bf16[64,1280]{1,0:T(8,128)(2,1)}, bf16[64,1280]{1,0:T(8,128)(2,1)}, bf16[1280,1024]{1,0:T(8,128)(2,1)}, bf16[1024,1280]{1,0:T(8,128)(2,1)}, f3...) custom-call(bf16[64,1280]{1,0:T(8,128)(2,1)} %bitcast.21, ...), custom_call_target="tpu_custom_call" | custom-call | flops 24159191040 | bytes 26214400 | tf_op jit(solution)/shard_map/pallas_call | solution.py:862
  220.5 10.9 %shard_map.153 = (bf16[64,1280]{1,0:T(8,128)(2,1)}, bf16[64,1280]{1,0:T(8,128)(2,1)}, bf16[1280,1024]{1,0:T(8,128)(2,1)}, bf16[1024,1280]{1,0:T(8,128)(2,1)}, f3...) custom-call(bf16[64,1280]{1,0:T(8,128)(2,1)} %get-tuple-element.24.refs_0_, ...), custom_call_target="tpu_custom_call" | custom-call | tf_op jit(solution)/shard_map/pallas_call | solution.py:833

commit v2 on v1

--- a/solution.py
+++ b/solution.py
@@ -295,11 +295,12 @@
         return low.at[s, col] if t == LOW else tok.at[t, s, col]
 
     def tok_z(t, d):
-        return remote(piece(t, z, c), piece(t, z, c), v.s_tz, (t, d), {SECTION: ahead(d)})
+        here = piece(t, behind(d - 1), c)
+        return remote(here, here, v.s_tz, (t, d), {SECTION: ahead(1)})
 
     def tok_z_in(t, d):
         here = piece(t, behind(d), c)
-        return remote(here, here, v.s_tz, (t, d), {SECTION: ahead(d)})
+        return remote(here, here, v.s_tz, (t, d), {SECTION: ahead(1)})
 
     def tok_y(t, d, g):
         here = piece(t, behind(d), c)
@@ -351,11 +352,7 @@
 
     def rs_z(j, d):
         zs, zr = sums(j)[3:]
-        return remote(zs.at[behind(d)], zr.at[z], v.s_rz, (j, d), {SECTION: behind(d)})
-
-    def rs_z_in(j, d):
-        here = sums(j)[4].at[ahead(d)]
-        return remote(here, here, v.s_rz, (j, d), {SECTION: behind(d)})
+        return remote(zs.at[d], zr.at[d], v.s_rz, (j, d), {SECTION: ahead(1)})
 
     def grad_slot(k, s, half):
         return (v.gl_in if k == 0 else v.gr_in).at[half, s]
@@ -417,10 +414,26 @@
 
     def forward(t, d):
         tok_z_in(t, d).wait_recv()
+
+        @pl.when(d + 1 < S)
+        def _():
+            tok_z(t, d + 1).start()
+
         spread(t, d)
 
-    def send(d):
-        for t in (BWD, COT):
+    def forward_all(d):
+        for t in (BWD, LOW, COT):
+            forward(t, d)
+
+        @pl.when(d + 1 < S)
+        def _():
+            for k in range(2):
+                fac(k, d + 1).start()
+
+        forward(FWD, d)
+
+    def send(d, low_too=True):
+        for t in (BWD, COT, LOW) if low_too else (BWD, COT):
             tok_z(t, d).start()
         for k in range(2):
             fac(k, d).start()
@@ -506,7 +519,7 @@
         v.gl_out[s, 0] = tn(mine[0, s], rank_tokens(COT, s)).astype(BF16)
         v.gr_out[s, 0] = tn(rank_tokens(BWD, s), mine[1, s]).astype(BF16)
 
-        @pl.when(d > 0)
+        @pl.when((d > 0) & (d + 2 >= S))
         def _():
             for k in range(2):
                 grad_z(k, d).start()
@@ -563,11 +576,17 @@
 
         @pl.when(d == 0)
         def _():
-            zr[z] = total.astype(BF16)
-
-        @pl.when(d > 0)
-        def _():
-            zs[s] = total.astype(BF16)
+            zr[0] = total.astype(BF16)
+
+        @pl.when(d == 1)
+        def _():
+            zs[1] = total.astype(BF16)
+            rs_z(j, 1).start()
+
+        @pl.when(d > 1)
+        def _():
+            rs_z(j, d - 1).wait_recv()
+            zs[d] = (total + zr[d - 1].astype(F32)).astype(BF16)
             rs_z(j, d).start()
 
     def pass_on(d):
@@ -577,12 +596,8 @@
 
     def home_sum(j):
         zr = sums(j)[4]
-        for d in range(1, S):
-            rs_z_in(j, d).wait_recv()
-        total = zr[0].astype(F32)
-        for s in range(1, S):
-            total = total + zr[s].astype(F32)
-        return total
+        rs_z(j, S - 1).wait_recv()
+        return zr[0].astype(F32) + zr[S - 1].astype(F32)
 
     def grad_up():
         step = min(TILE, units)
@@ -654,7 +669,7 @@
 
     spread(BWD, 0)
     spread(COT, 0)
-    send(1)
+    send(1, False)
     for copy in loads[3:5]:
         copy.wait()
     v.low_part[BWD] = nn(tok[BWD, z, c], ul[...]).astype(BF16)
@@ -668,58 +683,71 @@
             low[z, c, 2 * t + half] = (v.low_part[t, :, cols].astype(F32) + v.low_in[t, :, cols].astype(F32)).astype(BF16)
     low[z, c, 4] = (v.low_part[FWD, :, my_half].astype(F32) + v.low_in[FWD, :, my_half].astype(F32)).astype(BF16)
     spread(LOW, 0)
-    for d in range(1, S):
-        tok_z(LOW, d).start()
+    tok_z(LOW, 1).start()
     spread(FWD, 0)
     for copy in loads[5:]:
         copy.wait()
     bwd_partials(0, True)
     fwd_partials(0)
-    for t in (BWD, LOW, COT, FWD):
-        forward(t, 1)
-    send(2)
+    forward_all(1)
 
     @pl.loop(0, S)
     def _(i):
         @pl.when(i + 1 < S)
         def _():
             bwd_partials(i + 1, False)
-            fwd_partials(i + 1)
+
+        @pl.when(i + 1 == S)
+        def _():
+            @pl.loop(1, S)
+            def _(d):
+                fwd_partials(d)
 
         @pl.when(i > 0)
         def _():
             reduce_chunk(0, i - 1)
-            reduce_chunk(1, i - 1)
 
         bwd_chunk(i)
         reduce_core(0, i)
+
+        @pl.when(i == 0)
+        def _():
+            fwd_chunk(0)
+            reduce_core(1, 0)
+
+        @pl.when(i + 2 < S)
+        def _():
+            forward_all(i + 2)
+
+        @pl.when((i > 0) & (i + 2 < S))
+        def _():
+            for k in range(2):
+                grad_z(k, i).start()
+
+    reduce_chunk(0, S - 1)
+    grad_up()
+
+    @pl.loop(1, S)
+    def _(i):
         fwd_chunk(i)
         reduce_core(1, i)
-
-        @pl.when(i + 2 < S)
-        def _():
-            for t in (BWD, LOW, COT, FWD):
-                forward(t, i + 2)
-
-        @pl.when(i + 3 < S)
-        def _():
-            send(i + 3)
-
-        @pl.when(i > FULL)
-        def _():
-            pass_on(i - 1)
-
-    reduce_chunk(0, S - 1)
+        reduce_chunk(1, i - 1)
+
+        @pl.when((i >= FULL) & (i + 1 < S))
+        def _():
+            pass_on(i)
+
     reduce_chunk(1, S - 1)
-    grad_up()
-    if FULL < S:
-        pass_on(S - 1)
 
     total = home_sum(0)
     v.rank_out[0] = total[:, width : width + share].astype(BF16)
     v.rank_out[1] = total[:, width + share :].astype(BF16)
     rank_x(0).start()
     grad_norm = total[:, :width] + tok[COT, z, c].astype(F32)
+    total = home_sum(1)
+    v.rank_out[2] = total[:, width:].astype(BF16)
+    rank_x(1).start()
+    out = total[:, :width] + tok[FWD, z, c].astype(F32)
     rank_x(0).wait()
     v.rank_all[c, :, :, my_half] = v.rank_out[0:2]
     v.rank_all[c, :, :, other_half] = v.rank_in[0:2]
@@ -727,12 +755,12 @@
         rank_c(e).start()
     v.hand[0] = (grad_norm + nt(v.rank_all[c, 0], ul[...])).astype(BF16)
     hand(0).start()
-
-    grad_down()
-
-    total = home_sum(1)
-    v.rank_out[2] = total[:, width:].astype(BF16)
-    rank_x(1).start()
+    rank_x(1).wait()
+    out = out + nn(v.rank_out[2], dr[my_half, :]) + nn(v.rank_in[2], dr[other_half, :])
+    v.hand[1] = out.astype(BF16)
+    hand(1).start()
+    for d in range(S - 1, S):
+        pass_on(d)
     for e in range(1, C):
         rank_c_in(e).wait_recv()
     v.gul[...] = tn(tokens(BWD, z), v.rank_all[:, 0].reshape(micro, rank))
@@ -741,11 +769,7 @@
     v.gdr[...] = tn(v.rank_all[:, 1].reshape(micro, rank), tokens(COT, z))
     put_down = pltpu.make_async_copy(v.gdr, gdr_o, v.s_put.at[5])
     put_down.start()
-    rank_x(1).wait()
-    out = total[:, :width] + tok[FWD, z, c].astype(F32)
-    out = out + nn(v.rank_out[2], dr[my_half, :]) + nn(v.rank_in[2], dr[other_half, :])
-    v.hand[1] = out.astype(BF16)
-    hand(1).start()
+    grad_down()
 
     for k in range(2):
         for other in range(2):

time: 231 us -> 209 us (0.905)
  Pallas kernels: 231 us -> 208 us
    pallas_call x1, Pallas kernels: 220 us -> 197 us  [fused(): pl.pallas_call(functools.partial(kernel, S, C, list(shapes)), out_shape=[...]
where the time goes in v2:
time: 209 us
  Pallas kernels  208 us (100%)
    pallas_call x1, Pallas kernels, fused(): pl.pallas_call(functools.partial(kernel, S, C, list(shapes)), out_shape=[...  197 us
    pallas_call x1, Pallas kernels, finish(): pl.pallas_call(functools.partial(finish_kernel, count), out_shape=outs, i...  10.9 us

profile of v2, /device:TPU:0, one launch (start us, length us, event | category | flops | bytes accessed | tf_op | source)
XLA Modules:
  0.0 208.5 jit_solution(7527045734478179016)
XLA Ops:
  0.6 197.0 %shard_map.152 = (bf16[64,1280]{1,0:T(8,128)(2,1)}, bf16[64,1280]{1,0:T(8,128)(2,1)}, bf16[1280,1024]{1,0:T(8,128)(2,1)}, bf16[1024,1280]{1,0:T(8,128)(2,1)}, f3...) custom-call(bf16[64,1280]{1,0:T(8,128)(2,1)} %bitcast.21, ...), custom_call_target="tpu_custom_call" | custom-call | flops 24159191040 | bytes 26214400 | tf_op jit(solution)/shard_map/pallas_call | solution.py:886
  197.7 10.9 %shard_map.153 = (bf16[64,1280]{1,0:T(8,128)(2,1)}, bf16[64,1280]{1,0:T(8,128)(2,1)}, bf16[1280,1024]{1,0:T(8,128)(2,1)}, bf16[1024,1280]{1,0:T(8,128)(2,1)}, f3...) custom-call(bf16[64,1280]{1,0:T(8,128)(2,1)} %get-tuple-element.24.refs_0_, ...), custom_call_target="tpu_custom_call" | custom-call | tf_op jit(solution)/shard_map/pallas_call | solution.py:857

commit v3 on v2

--- a/solution.py
+++ b/solution.py
@@ -508,6 +508,30 @@
             mine[0, s, :, cols] = (p * sigma).astype(BF16)
             mine[1, s, :, cols] = (g * (sigma * (1.0 + p * (1.0 - sigma)))).astype(BF16)
 
+        v.gl_out[s, 0] = tn(mine[0, s], rank_tokens(COT, s)).astype(BF16)
+        v.gr_out[s, 0] = tn(rank_tokens(BWD, s), mine[1, s]).astype(BF16)
+
+        @pl.when((d > 0) & (d + 2 >= S))
+        def _():
+            for k in range(2):
+                grad_z(k, d).start()
+
+        @pl.when(d < FULL)
+        def _():
+            v.gl_out[s, 1] = tn(mine[0, s], rank_tokens(COT, s, 1 - r)).astype(BF16)
+            v.gr_out[s, 1] = tn(rank_tokens(BWD, s, 1 - r), mine[1, s]).astype(BF16)
+
+        @pl.when((d < FULL) & (d > 0))
+        def _():
+            for k in range(2):
+                grad_z(k, d, 1).start()
+
+        @pl.when(d == 0)
+        def _():
+            for k in range(2):
+                for other in range(2):
+                    grad_keep(k, other).start()
+
         @pl.loop(0, width // TILE)
         def _(n):
             cols = at(n, TILE)
@@ -516,29 +540,6 @@
         by_owner(v.rs_b, s, slice(width, width + share), nt(mine[1, s], rt[s]))
         by_owner(v.rs_b, s, slice(width + share, width + 2 * share), nn(mine[0, s], lt[s]))
         rs_k(0, d).start()
-        v.gl_out[s, 0] = tn(mine[0, s], rank_tokens(COT, s)).astype(BF16)
-        v.gr_out[s, 0] = tn(rank_tokens(BWD, s), mine[1, s]).astype(BF16)
-
-        @pl.when((d > 0) & (d + 2 >= S))
-        def _():
-            for k in range(2):
-                grad_z(k, d).start()
-
-        @pl.when(d < FULL)
-        def _():
-            v.gl_out[s, 1] = tn(mine[0, s], rank_tokens(COT, s, 1 - r)).astype(BF16)
-            v.gr_out[s, 1] = tn(rank_tokens(BWD, s, 1 - r), mine[1, s]).astype(BF16)
-
-        @pl.when((d < FULL) & (d > 0))
-        def _():
-            for k in range(2):
-                grad_z(k, d, 1).start()
-
-        @pl.when(d == 0)
-        def _():
-            for k in range(2):
-                for other in range(2):
-                    grad_keep(k, other).start()
 
     def fwd_chunk(d):
         s = behind(d)

time: 209 us -> 209 us (level)
  no operation moved by 1% of the time
where the time goes in v3:
time: 209 us
  Pallas kernels  208 us (100%)
    pallas_call x1, Pallas kernels, fused(): pl.pallas_call(functools.partial(kernel, S, C, list(shapes)), out_shape=[...  197 us
    pallas_call x1, Pallas kernels, finish(): pl.pallas_call(functools.partial(finish_kernel, count), out_shape=outs, i...  10.9 us

profile of v3, /device:TPU:0, one launch (start us, length us, event | category | flops | bytes accessed | tf_op | source)
XLA Modules:
  0.0 208.5 jit_solution(2532743373365150934)
XLA Ops:
  0.6 197.0 %shard_map.152 = (bf16[64,1280]{1,0:T(8,128)(2,1)}, bf16[64,1280]{1,0:T(8,128)(2,1)}, bf16[1280,1024]{1,0:T(8,128)(2,1)}, bf16[1024,1280]{1,0:T(8,128)(2,1)}, f3...) custom-call(bf16[64,1280]{1,0:T(8,128)(2,1)} %bitcast.21, ...), custom_call_target="tpu_custom_call" | custom-call | flops 24159191040 | bytes 26214400 | tf_op jit(solution)/shard_map/pallas_call | solution.py:887
  197.7 10.9 %shard_map.153 = (bf16[64,1280]{1,0:T(8,128)(2,1)}, bf16[64,1280]{1,0:T(8,128)(2,1)}, bf16[1280,1024]{1,0:T(8,128)(2,1)}, bf16[1024,1280]{1,0:T(8,128)(2,1)}, f3...) custom-call(bf16[64,1280]{1,0:T(8,128)(2,1)} %get-tuple-element.24.refs_0_, ...), custom_call_target="tpu_custom_call" | custom-call | tf_op jit(solution)/shard_map/pallas_call | solution.py:858
